TPU v7x, 32 devices: a whole 2x2x4 slice. The times are simulated.
32 devices in a mesh: ctx: 8 (over z, x), head: 4 (over y, core).
Axes of the slice: x: 2, y: 2, z: 4, core: 2. Of those that a mesh axis runs over, the one named last changes fastest.
Arguments:
- hidden: bfloat16 [256, 8192], P(None, 'ctx')
- norm_gain: float32 [8192], replicated, may hold values from 0.1 to 1.9
- w_query: bfloat16 [8192, 8192], P('ctx', 'head'), may hold values from -0.0625 to 0.0625
- manifest_keys: bfloat16 [8, 4096, 128], P(None, 'ctx')
- manifest_values: bfloat16 [8, 4096, 128], P(None, 'ctx'), may hold values from -6 to 6
- w_output: bfloat16 [8192, 8192], P('head', 'ctx'), may hold values from -0.0625 to 0.0625
- valid_len: int32 [256], replicated, may hold values from 1 to 4096, as said below
- home_block: int32 [256], replicated, may hold values from 0 to 7, as said below
Outputs:
- projected: float32 [256, 8192], P('head', 'ctx')
Inputs may be any that keep to these rules, and one draw needn't show every extreme that they name: `valid_len`: every draw has a row that reads the whole manifest and a row with length 1. `home_block`: every draw assigns some row to the first block and some row to the last.
All inputs are finite; a program needn't handle non-finite values.
Results may differ from a plain program's by a relative error of at most 0.005.
The roundings to bfloat16 on the way count: a program that leaves them out, or rounds other values in their place, can miss the bound.
Values may be sent and summed in bfloat16 or wider, within the bound.
A program may use at most 128 MiB of HBM per device.

v0:
```python
import math
import jax
import jax.numpy as jnp
from jax import lax
from jax.sharding import PartitionSpec as P

H = 64
KVH = 8
HD = 128


def shards(
    hidden, norm_gain, w_query, manifest_keys, manifest_values, w_output, valid_len, home_block
):
    ctx_count = lax.axis_size("ctx")
    ctx_index = lax.axis_index("ctx")
    head_index = lax.axis_index("head")
    rows, feat = hidden.shape
    d_model = feat * ctx_count
    width = w_query.shape[1]
    heads_here = width // HD
    group = H // KVH
    span = manifest_keys.shape[1]
    hsplit = min(ctx_count, heads_here)
    rsplit = ctx_count // hsplit
    rows_dev = rows // rsplit
    heads_dev = heads_here // hsplit
    widened = hidden.astype(jnp.float32)
    total_sq = lax.psum(jnp.sum(widened * widened, axis=1, keepdims=True), "ctx")
    inv_rms = lax.rsqrt(total_sq / d_model + 1e-05)
    gain = lax.dynamic_slice_in_dim(norm_gain, ctx_index * feat, feat, 0)
    normed = (widened * inv_rms * gain[None, :]).astype(jnp.bfloat16)
    partial = jnp.dot(normed, w_query, preferred_element_type=jnp.float32)
    partial = partial.reshape(rsplit, rows_dev, hsplit, heads_dev * HD).transpose(2, 0, 1, 3)
    partial = partial.reshape(ctx_count, rows_dev, heads_dev * HD)
    query = lax.psum_scatter(partial, "ctx", scatter_dimension=0, tiled=False).astype(jnp.bfloat16)
    dest_heads = head_index * heads_here + jnp.arange(ctx_count) // rsplit * heads_dev
    dest_kv = dest_heads // group
    kv = jnp.stack([manifest_keys[dest_kv], manifest_values[dest_kv]], axis=1)
    kv = lax.all_to_all(kv, "ctx", split_axis=0, concat_axis=0, tiled=True)
    kv = kv.transpose(1, 0, 2, 3).reshape(2, ctx_count * span, HD)
    keys, values = (kv[0], kv[1])
    first_row = ctx_index % rsplit * rows_dev
    lens = lax.dynamic_slice_in_dim(valid_len, first_row, rows_dev, 0)
    blocks = lax.dynamic_slice_in_dim(home_block, first_row, rows_dev, 0)
    places = jnp.arange(ctx_count * span, dtype=jnp.int32)
    usable = (places[None, :] < lens[:, None]) | ((places // span)[None, :] == blocks[:, None])
    usable = usable[:, None, :]
    q3 = query.reshape(rows_dev, heads_dev, HD)
    scores = jnp.einsum("nhd,jd->nhj", q3, keys, preferred_element_type=jnp.float32) * (
        1.0 / math.sqrt(HD)
    )
    scores = jnp.where(usable, scores, -1e30)
    row_max = jnp.max(scores, axis=2, keepdims=True)
    expo = jnp.where(usable, jnp.exp(scores - row_max), 0.0)
    row_sum = jnp.sum(expo, axis=2, keepdims=True)
    weighted = jnp.einsum(
        "nhj,jd->nhd", expo.astype(jnp.bfloat16), values, preferred_element_type=jnp.float32
    )
    attn = (weighted / row_sum).astype(jnp.bfloat16).reshape(rows_dev, heads_dev * HD)
    attn = lax.all_gather(attn, "ctx", axis=0, tiled=False)
    attn = attn.reshape(hsplit, rsplit, rows_dev, heads_dev * HD).transpose(1, 2, 0, 3)
    attn = attn.reshape(rows, width)
    return lax.psum_scatter(
        jnp.dot(attn, w_output, preferred_element_type=jnp.float32),
        "head",
        scatter_dimension=0,
        tiled=True,
    )


def solution(mesh):
    in_specs = (
        P(None, "ctx"),
        P(),
        P("ctx", "head"),
        P(None, "ctx", None),
        P(None, "ctx", None),
        P("head", "ctx"),
        P(),
        P(),
    )
    out_specs = P("head", "ctx")
    return jax.shard_map(shards, mesh=mesh, in_specs=in_specs, out_specs=out_specs, check_vma=False)
```

profile of v0, /device:TPU:0, one launch (start us, length us, event | category | flops | bytes accessed | tf_op | source)
XLA Modules:
  0.0 222.7 jit_solution(15778530597544170264)
XLA Ops:
  6.5 0.0 copy-start
  6.5 0.0 reduce-scatter.3.cloned.1.call-start
  6.5 1.3 fusion.14
  7.9 23.1 %psum.7 = f32[256,1]{0,1:T(1,128)S(1)} all-reduce(f32[256,1]{0,1:T(1,128)S(1)} %bitcast.42), channel_id=1, replica_groups=mesh['ctx'=8,'head'=4] {'ctx'}, use_global_device_ids=true, to_apply=%region_1.0 | all-reduce | flops 256 | bytes 2048 | tf_op jit(solution)/shard_map/psum | solution.py:29
  31.0 0.7 dynamic_slice.2
  31.6 5.5 %fusion.19 = f32[256,2048]{0,1:T(8,128)} fusion(bf16[1024,2048]{1,0:T(8,128)(2,1)} %param.10, bf16[256,1024]{1,0:T(8,128)(2,1)} %param.8, f32[1024]{0:T(1024)S(1)} %dynamic_slice.2, f32[256]{0:T(256)S(1)} %bitcast.43), kind=kOutput, calls=%fused_computation.22 | convolution fusion | flops 1074790400 | bytes 6820864 | tf_op jit(solution)/shard_map/reshape | solution.py:34
  37.2 0.0 reduce-scatter.3.cloned.1.call-update
  37.2 0.0 copy-done
  37.2 0.7 gather_fusion.1
  38.0 2.0 gather_fusion
  40.0 0.0 copy-start.2
  40.0 0.0 copy-start.3
  40.0 1.5 pad_maximum_fusion
  41.5 3.6 %all-to-all-start = ((bf16[8,2,512,128]{3,2,1,0:T(8,128)(2,1)}), bf16[8,2,512,128]{3,2,1,0:T(8,128)(2,1)S(1)}, u32[]{:S(2)}, u32[]{:S(2)}) async-start(bf16[8,2,512,128]{3,2,1,0:T(8,128)(2,1)} %pad_maximum_fusion), calls=%async_computation.1 | async-start | bytes 4194304 | tf_op jit(solution)/shard_map/all_to_all | solution.py:40
  45.1 0.0 all-gather.2.cloned.1.call-start
  45.1 0.0 copy-done.2
  45.2 0.0 copy-done.3
  45.2 1.9 fusion.6
  47.0 59.5 %all-to-all-done = bf16[8,2,512,128]{3,2,1,0:T(8,128)(2,1)S(1)} async-done(((bf16[8,2,512,128]{3,2,1,0:T(8,128)(2,1)}), bf16[8,2,512,128]{3,2,1,0:T(8,128)(2,1)S(1)}, u32[]{:S(2)}, u32[]{:S(2)}) %all-to-all-start) | async-done | bytes 2097184 | tf_op jit(solution)/shard_map/all_to_all | solution.py:40
  106.5 1.5 fusion.29
  108.0 25.2 %reduce-scatter.3.cloned.1.call-done = f32[1,256,256]{1,2,0:T(8,128)} async-done(((f32[8,256,256]{1,2,0:T(8,128)}), f32[1,256,256]{1,2,0:T(8,128)}) %reduce-scatter.3.cloned.1.call-update) | async-done | bytes 262160 | tf_op jit(solution)/shard_map/reduce_scatter | solution.py:36
  133.2 1.0 convert_element_type.21
  134.2 8.3 %fusion.30 = (f32[256,2]{0,1:T(2,128)S(1)}, bf16[256,2,4096]{2,0,1:T(8,128)(2,1)}) fusion(pred[256,4096]{1,0:T(8,128)(4,1)} %fusion.6, bf16[256,2,128]{0,2,1:T(8,128)(2,1)S(1)} %bitcast.41, bf16[4096,128,1]{1,0,2:T(8,128)(2,1)} %bitcast.39), kind=kOutput, calls=%fused_computation.43 | convolution fusion | flops 549457920 | bytes 6424576 | tf_op jit(solution)/shard_map/sub | solution.py:55
  142.5 3.7 %fusion.11 = bf16[256,2,128]{0,2,1:T(8,128)(2,1)S(1)} fusion(bf16[4096,128,1]{1,0,2:T(8,128)(2,1)S(1)} %bitcast.34, bf16[256,2,4096]{2,0,1:T(8,128)(2,1)} %get-tuple-element.8, f32[256,2]{0,1:T(2,128)S(1)} %get-tuple-element.7), kind=kOutput, calls=%fused_computation.17 | convolution fusion | flops 537001984 | bytes 5376000 | tf_op jit(solution)/shard_map/nhj,jd->nhd/dot_general | solution.py:57
  146.2 0.8 copy.20
  146.9 0.0 all-gather.2.cloned.1.call-update
  147.0 0.0 reduce-scatter.5.cloned.1.call-start
  147.0 39.4 %all-gather.2.cloned.1.call-done = bf16[8,256,256]{2,1,0:T(8,128)(2,1)} async-done(((bf16[1,256,256]{2,1,0:T(8,128)(2,1)}), bf16[8,256,256]{2,1,0:T(8,128)(2,1)}) %all-gather.2.cloned.1.call-update) | async-done | bytes 1048592 | tf_op jit(solution)/shard_map/all_gather | solution.py:61
  186.4 1.5 copy.21
  187.9 4.5 %fusion.31 = f32[256,1024]{1,0:T(8,128)} fusion(bf16[256,2048]{0,1:T(8,128)(2,1)S(1)} %bitcast.38, bf16[2048,1024]{1,0:T(8,128)(2,1)} %param.13), kind=kOutput, calls=%fused_computation.44 | convolution fusion | flops 1073741824 | bytes 6291456 | tf_op jit(solution)/shard_map/dot_general | solution.py:65
  192.4 0.0 reduce-scatter.5.cloned.1.call-update
  192.4 23.8 %reduce-scatter.5.cloned.1.call-done = f32[64,1024]{1,0:T(8,128)} async-done(((f32[256,1024]{1,0:T(8,128)}), f32[64,1024]{1,0:T(8,128)}) %reduce-scatter.5.cloned.1.call-update) | async-done | bytes 262160 | tf_op jit(solution)/shard_map/reduce_scatter | solution.py:64
  (6 shorter events, 0.0 us)
Async XLA Ops:
  6.5 30.7 %copy-start = (bf16[8,512,128]{2,1,0:T(8,128)(2,1)S(1)}, bf16[8,512,128]{2,1,0:T(8,128)(2,1)}, u32[]{:S(2)}) copy-start(bf16[8,512,128]{2,1,0:T(8,128)(2,1)} %param.12) | copy-start | bytes 3145732
  6.5 126.7 %reduce-scatter.3.cloned.1.call-start = ((), (), s32[]{:S(2)}) async-start(), calls=%async_computation.3 | async-start | bytes 2359296 | tf_op jit(solution)/shard_map/reduce_scatter | solution.py:36
  40.0 5.2 %copy-start.2 = (s32[256]{0:T(256)S(1)}, s32[256]{0:T(256)}, u32[]{:S(2)}) copy-start(s32[256]{0:T(256)} %param.14) | copy-start | bytes 3076
  40.0 5.2 %copy-start.3 = (s32[256]{0:T(256)S(1)}, s32[256]{0:T(256)}, u32[]{:S(2)}) copy-start(s32[256]{0:T(256)} %param.15) | copy-start | bytes 3076
  41.5 65.0 %all-to-all-start = ((bf16[8,2,512,128]{3,2,1,0:T(8,128)(2,1)}), bf16[8,2,512,128]{3,2,1,0:T(8,128)(2,1)S(1)}, u32[]{:S(2)}, u32[]{:S(2)}) async-start(bf16[8,2,512,128]{3,2,1,0:T(8,128)(2,1)} %pad_maximum_fusion), calls=%async_computation.1 | async-start | bytes 4194304 | tf_op jit(solution)/shard_map/all_to_all | solution.py:40
  45.1 141.3 %all-gather.2.cloned.1.call-start = ((), (), s32[]{:S(2)}) async-start(), calls=%async_computation.4 | async-start | bytes 1179648 | tf_op jit(solution)/shard_map/all_gather | solution.py:61
  134.2 8.3 %copy-start.1 = (bf16[1,8,512,128]{3,2,0,1:T(8,128)(2,1)S(1)}, bf16[1,8,512,128]{3,2,0,1:T(8,128)(2,1)}, u32[]{:S(2)}) copy-start(bf16[1,8,512,128]{3,2,0,1:T(8,128)(2,1)} %get-tuple-element.6) | copy-start | bytes 3145732
  147.0 69.2 %reduce-scatter.5.cloned.1.call-start = ((), (), s32[]{:S(2)}) async-start(), calls=%async_computation.5 | async-start | bytes 1310720 | tf_op jit(solution)/shard_map/reduce_scatter | solution.py:64
Sparse Core Ops, SparseCore 0:
  37.3 95.8 reduce-scatter.2
  147.1 39.2 all-gather.1
  192.5 23.6 reduce-scatter.4
where the time goes:
time: 223 us
  waiting for transfers between devices  148 us (66%)
  blocking collectives  23.1 us (10%)
  matrix products  22 us (10%)
  between operations  13.2 us (6%)
  local copies, waits for them, and re-layouts  7.19 us (3%)
  other arithmetic  5.66 us (3%)
  starting transfers between devices  3.69 us (2%)
    all_to_all x1, waiting for transfers between devices, shards(): kv = lax.all_to_all(kv, 'ctx', split_axis=0, concat_axis=0, tiled=True)  59.5 us
    all_gather x1, waiting for transfers between devices, shards(): attn = lax.all_gather(attn, 'ctx', axis=0, tiled=False)  39.4 us
    reduce_scatter x1, waiting for transfers between devices, shards(): lax.psum_scatter(partial, 'ctx', scatter_dimension=0, tiled=False)  25.2 us
    reduce_scatter x1, waiting for transfers between devices, shards(): lax.psum_scatter(jnp.dot(attn, w_output, preferred_element_type=jnp.float...  23.8 us
    psum x1, blocking collectives, shards(): lax.psum(jnp.sum(widened * widened, axis=1, keepdims=True), 'ctx')  23.1 us
    sub x1, matrix products, shards(): expo = jnp.where(usable, jnp.exp(scores - row_max), 0.0)  8.3 us
    reshape x1, matrix products, shards(): partial.reshape(rsplit, rows_dev, hsplit, heads_dev * HD)  5.51 us
    dot_general x1, matrix products, shards(): jnp.dot(attn, w_output, preferred_element_type=jnp.float32)  4.46 us
  transfers between devices with their start and end apart: 4, of which 4 were waited for; matrix products, arithmetic and copies ran while one was open for 3% of the time, Pallas kernels for 0%

commit v1 on v0

--- a/solution.py
+++ b/solution.py
@@ -26,7 +26,9 @@
     rows_dev = rows // rsplit
     heads_dev = heads_here // hsplit
     widened = hidden.astype(jnp.float32)
-    total_sq = lax.psum(jnp.sum(widened * widened, axis=1, keepdims=True), "ctx")
+    total_sq = jnp.sum(
+        lax.all_gather(jnp.sum(widened * widened, axis=1, keepdims=True), "ctx"), axis=0
+    )
     inv_rms = lax.rsqrt(total_sq / d_model + 1e-05)
     gain = lax.dynamic_slice_in_dim(norm_gain, ctx_index * feat, feat, 0)
     normed = (widened * inv_rms * gain[None, :]).astype(jnp.bfloat16)

time: 223 us -> 222 us (level)
    psum x1 -> x0, blocking collectives: 23.1 us -> none  [shards(): lax.psum(jnp.sum(widened * widened, axis=1, keepdims=True), 'ctx')]
    all_gather x0 -> x1, blocking collectives: none -> 22.2 us  [shards(): lax.all_gather(jnp.sum(widened * widened, axis=1, keepdims=True), 'ctx')]
where the time goes in v1:
time: 222 us
  waiting for transfers between devices  148 us (67%)
  blocking collectives  22.2 us (10%)
  matrix products  22 us (10%)
  between operations  13.2 us (6%)
  local copies, waits for them, and re-layouts  7.18 us (3%)
  other arithmetic  5.69 us (3%)
  starting transfers between devices  3.69 us (2%)
    all_to_all x1, waiting for transfers between devices, shards(): kv = lax.all_to_all(kv, 'ctx', split_axis=0, concat_axis=0, tiled=True)  59.5 us
    all_gather x1, waiting for transfers between devices, shards(): attn = lax.all_gather(attn, 'ctx', axis=0, tiled=False)  39.4 us
    reduce_scatter x1, waiting for transfers between devices, shards(): lax.psum_scatter(partial, 'ctx', scatter_dimension=0, tiled=False)  25.2 us
    reduce_scatter x1, waiting for transfers between devices, shards(): lax.psum_scatter(jnp.dot(attn, w_output, preferred_element_type=jnp.float...  23.8 us
    all_gather x1, blocking collectives, shards(): lax.all_gather(jnp.sum(widened * widened, axis=1, keepdims=True), 'ctx')  22.2 us
    sub x1, matrix products, shards(): expo = jnp.where(usable, jnp.exp(scores - row_max), 0.0)  8.3 us
    reshape x1, matrix products, shards(): partial.reshape(rsplit, rows_dev, hsplit, heads_dev * HD)  5.51 us
    dot_general x1, matrix products, shards(): jnp.dot(attn, w_output, preferred_element_type=jnp.float32)  4.46 us
  transfers between devices with their start and end apart: 4, of which 4 were waited for; matrix products, arithmetic and copies ran while one was open for 3% of the time, Pallas kernels for 0%

profile of v1, /device:TPU:0, one launch (start us, length us, event | category | flops | bytes accessed | tf_op | source)
XLA Modules:
  0.0 221.9 jit_solution(16769434317280432649)
XLA Ops:
  6.5 0.0 copy-start
  6.5 0.0 reduce-scatter.3.cloned.1.call-start
  6.5 1.3 fusion.14
  7.9 22.2 %all-gather.1 = f32[8,1,256]{2,1,0:T(1,128)S(1)} all-gather(f32[1,1,256]{2,1,0:T(1,128)S(1)} %bitcast.41), channel_id=2, replica_groups=mesh['ctx'=8,'head'=4] {'ctx'}, dimensions={0}, use_global_device_ids=true | all-gather | bytes 9216 | tf_op jit(solution)/shard_map/all_gather | solution.py:30
  30.1 0.7 dynamic_slice.2
  30.8 5.5 %fusion.19 = f32[256,2048]{0,1:T(8,128)} fusion(bf16[1024,2048]{1,0:T(8,128)(2,1)} %param.10, bf16[256,1024]{1,0:T(8,128)(2,1)} %param.8, f32[1024]{0:T(1024)S(1)} %dynamic_slice.2, f32[256]{0:T(256)S(1)} %add_rsqrt_fusion), kind=kOutput, calls=%fused_computation.22 | convolution fusion | flops 1074790400 | bytes 6820864 | tf_op jit(solution)/shard_map/reshape | solution.py:36
  36.3 0.0 reduce-scatter.3.cloned.1.call-update
  36.4 0.0 copy-done
  36.4 0.7 gather_fusion.1
  37.2 2.0 gather_fusion
  39.1 0.0 copy-start.2
  39.1 0.0 copy-start.3
  39.2 1.5 pad_maximum_fusion
  40.6 3.6 %all-to-all-start = ((bf16[8,2,512,128]{3,2,1,0:T(8,128)(2,1)}), bf16[8,2,512,128]{3,2,1,0:T(8,128)(2,1)S(1)}, u32[]{:S(2)}, u32[]{:S(2)}) async-start(bf16[8,2,512,128]{3,2,1,0:T(8,128)(2,1)} %pad_maximum_fusion), calls=%async_computation.1 | async-start | bytes 4194304 | tf_op jit(solution)/shard_map/all_to_all | solution.py:42
  44.2 0.0 all-gather.4.cloned.1.call-start
  44.3 0.0 copy-done.2
  44.3 1.9 fusion.6
  46.2 59.5 %all-to-all-done = bf16[8,2,512,128]{3,2,1,0:T(8,128)(2,1)S(1)} async-done(((bf16[8,2,512,128]{3,2,1,0:T(8,128)(2,1)}), bf16[8,2,512,128]{3,2,1,0:T(8,128)(2,1)S(1)}, u32[]{:S(2)}, u32[]{:S(2)}) %all-to-all-start) | async-done | bytes 2097184 | tf_op jit(solution)/shard_map/all_to_all | solution.py:42
  105.7 1.5 fusion.29
  107.2 25.2 %reduce-scatter.3.cloned.1.call-done = f32[1,256,256]{1,2,0:T(8,128)} async-done(((f32[8,256,256]{1,2,0:T(8,128)}), f32[1,256,256]{1,2,0:T(8,128)}) %reduce-scatter.3.cloned.1.call-update) | async-done | bytes 262160 | tf_op jit(solution)/shard_map/reduce_scatter | solution.py:38
  132.4 1.0 convert_element_type.21
  133.4 0.0 copy-start.1
  133.4 8.3 %fusion.30 = (f32[256,2]{0,1:T(2,128)S(1)}, bf16[256,2,4096]{2,0,1:T(8,128)(2,1)}) fusion(pred[256,4096]{1,0:T(8,128)(4,1)} %fusion.6, bf16[256,2,128]{0,2,1:T(8,128)(2,1)S(1)} %bitcast.40, bf16[4096,128,1]{1,0,2:T(8,128)(2,1)} %bitcast.38), kind=kOutput, calls=%fused_computation.43 | convolution fusion | flops 549457920 | bytes 6424576 | tf_op jit(solution)/shard_map/sub | solution.py:57
  141.7 3.7 %fusion.11 = bf16[256,2,128]{0,2,1:T(8,128)(2,1)S(1)} fusion(bf16[4096,128,1]{1,0,2:T(8,128)(2,1)S(1)} %bitcast.33, bf16[256,2,4096]{2,0,1:T(8,128)(2,1)} %get-tuple-element.8, f32[256,2]{0,1:T(2,128)S(1)} %get-tuple-element.7), kind=kOutput, calls=%fused_computation.17 | convolution fusion | flops 537001984 | bytes 5376000 | tf_op jit(solution)/shard_map/nhj,jd->nhd/dot_general | solution.py:59
  145.4 0.8 copy.20
  146.2 0.0 all-gather.4.cloned.1.call-update
  146.2 0.0 reduce-scatter.5.cloned.1.call-start
  146.2 39.4 %all-gather.4.cloned.1.call-done = bf16[8,256,256]{2,1,0:T(8,128)(2,1)} async-done(((bf16[1,256,256]{2,1,0:T(8,128)(2,1)}), bf16[8,256,256]{2,1,0:T(8,128)(2,1)}) %all-gather.4.cloned.1.call-update) | async-done | bytes 1048592 | tf_op jit(solution)/shard_map/all_gather | solution.py:63
  185.6 1.5 copy.21
  187.1 4.5 %fusion.31 = f32[256,1024]{1,0:T(8,128)} fusion(bf16[256,2048]{0,1:T(8,128)(2,1)S(1)} %bitcast.37, bf16[2048,1024]{1,0:T(8,128)(2,1)} %param.13), kind=kOutput, calls=%fused_computation.44 | convolution fusion | flops 1073741824 | bytes 6291456 | tf_op jit(solution)/shard_map/dot_general | solution.py:67
  191.5 0.0 reduce-scatter.5.cloned.1.call-update
  191.6 23.8 %reduce-scatter.5.cloned.1.call-done = f32[64,1024]{1,0:T(8,128)} async-done(((f32[256,1024]{1,0:T(8,128)}), f32[64,1024]{1,0:T(8,128)}) %reduce-scatter.5.cloned.1.call-update) | async-done | bytes 262160 | tf_op jit(solution)/shard_map/reduce_scatter | solution.py:66
  (7 shorter events, 0.1 us)
Async XLA Ops:
  6.5 29.9 %copy-start = (bf16[8,512,128]{2,1,0:T(8,128)(2,1)S(1)}, bf16[8,512,128]{2,1,0:T(8,128)(2,1)}, u32[]{:S(2)}) copy-start(bf16[8,512,128]{2,1,0:T(8,128)(2,1)} %param.12) | copy-start | bytes 3145732
  6.5 125.9 %reduce-scatter.3.cloned.1.call-start = ((), (), s32[]{:S(2)}) async-start(), calls=%async_computation.3 | async-start | bytes 2359296 | tf_op jit(solution)/shard_map/reduce_scatter | solution.py:38
  39.1 5.2 %copy-start.2 = (s32[256]{0:T(256)S(1)}, s32[256]{0:T(256)}, u32[]{:S(2)}) copy-start(s32[256]{0:T(256)} %param.14) | copy-start | bytes 3076
  39.1 5.2 %copy-start.3 = (s32[256]{0:T(256)S(1)}, s32[256]{0:T(256)}, u32[]{:S(2)}) copy-start(s32[256]{0:T(256)} %param.15) | copy-start | bytes 3076
  40.6 65.0 %all-to-all-start = ((bf16[8,2,512,128]{3,2,1,0:T(8,128)(2,1)}), bf16[8,2,512,128]{3,2,1,0:T(8,128)(2,1)S(1)}, u32[]{:S(2)}, u32[]{:S(2)}) async-start(bf16[8,2,512,128]{3,2,1,0:T(8,128)(2,1)} %pad_maximum_fusion), calls=%async_computation.1 | async-start | bytes 4194304 | tf_op jit(solution)/shard_map/all_to_all | solution.py:42
  44.2 141.3 %all-gather.4.cloned.1.call-start = ((), (), s32[]{:S(2)}) async-start(), calls=%async_computation.4 | async-start | bytes 1179648 | tf_op jit(solution)/shard_map/all_gather | solution.py:63
  133.4 8.3 %copy-start.1 = (bf16[1,8,512,128]{3,2,0,1:T(8,128)(2,1)S(1)}, bf16[1,8,512,128]{3,2,0,1:T(8,128)(2,1)}, u32[]{:S(2)}) copy-start(bf16[1,8,512,128]{3,2,0,1:T(8,128)(2,1)} %get-tuple-element.6) | copy-start | bytes 3145732
  146.2 69.2 %reduce-scatter.5.cloned.1.call-start = ((), (), s32[]{:S(2)}) async-start(), calls=%async_computation.5 | async-start | bytes 1310720 | tf_op jit(solution)/shard_map/reduce_scatter | solution.py:66
Sparse Core Ops, SparseCore 0:
  36.5 95.8 reduce-scatter.2
  146.3 39.2 all-gather.3
  191.7 23.6 reduce-scatter.4
